TPU v7x, 32 devices: a whole 2x2x4 slice. The times are simulated.
32 devices in a mesh: dp: 4 (over y, core), cells: 8 (over z, x).
Axes of the slice: x: 2, y: 2, z: 4, core: 2. Of those that a mesh axis runs over, the one named last changes fastest.
Arguments:
- sensitivity: float32 [8192, 12288], P('dp', 'cells'), may hold values from -0.0546875 to 0.0546875
- observed: float32 [8192, 256], P('dp'), may hold values from -6 to 6
- models: float32 [12288, 256], P('cells'), may hold values from -6 to 6
- neighbour_map: int32 [4, 768], replicated, may hold values from 0 to 767, as said below
- edge_mask: int32 [12288], P('cells'), may hold values 0 or 1
Outputs:
- updated: float32 [12288, 256], P('cells')
Inputs may be any that keep to these rules, and one draw needn't show every extreme that they name: `neighbour_map`: each row k maps every cell of a periodic 32 by 24 plane grid, numbered in a drawn order, to its neighbour in one of the four grid directions; every row is a permutation.
All inputs are finite; a program needn't handle non-finite values. No bound on the sum of `edge_mask` on one device may be relied on, other than what follows from the above.
Results may differ from a plain program's by a relative error of at most 0.0001.
Values sent between devices are 32-bit elements; how exact they have to be, the bound alone decides.
A program may use at most 128 MiB of HBM per device.

v0:
```python
import functools

import jax
import jax.numpy as jnp
from jax import lax
from jax.experimental import pallas as pl
from jax.experimental.pallas import tpu as pltpu
from jax.sharding import PartitionSpec as P

ITERS = 2
CHUNK = 256
PARTS = 1
HALVES = 2
LAG = 3
DP_LAG = 3
RADIX = 2
F32 = jnp.float32
BF16 = jnp.bfloat16


def split(x):
    hi = x.astype(BF16)
    return hi, (x - hi.astype(F32)).astype(BF16)


def digits_of(count, first):
    digits = []
    while count > 1:
        digits.append(first if not digits else min(RADIX, count))
        count //= digits[-1]
    return digits


def radix(n_dp, n_cells):
    return digits_of(n_dp, 2), digits_of(n_cells, 2)


def dot(a, b, dims):
    return lax.dot_general(a, b, (dims, ((), ())), preferred_element_type=F32)


def aligned(start, size):
    return pl.ds(pl.multiple_of(start, 8), size)


class Scatter:
    def __init__(self, axis, digits, rows, sends, recvs):
        self.axis, self.rows, self.digits = axis, rows, digits
        self.sends, self.recvs = sends, recvs
        self.levels = len(digits)
        self.stages = 2 * self.levels
        me = lax.axis_index(axis)
        self.peer, self.away, self.off, self.size, self.sem = [], [], [0], [rows], []
        stride, sem = 1, 0
        for b, base in enumerate(digits):
            mine = (me // stride) % base
            piece = self.size[b] // base
            others = [(mine + j) % base for j in range(1, base)]
            self.peer.append([me + (v - mine) * stride for v in others])
            self.away.append([self.off[b] + v * piece for v in others])
            self.off.append(self.off[b] + mine * piece)
            self.size.append(piece)
            self.sem.append(sem)
            sem += base - 1
            stride *= base
        self.copies = sem

    def kept(self, chunk, b):
        return aligned(chunk * self.rows + self.off[b + 1], self.size[b + 1])

    def landed(self, chunk, b, j):
        at = self.rows - self.size[b] + j * self.size[b + 1]
        return aligned(chunk * self.rows + at, self.size[b + 1])

    def remote(self, source, target, slot, sem, peer):
        return pltpu.make_async_remote_copy(
            src_ref=source,
            dst_ref=target,
            send_sem=self.sends.at[sem, slot],
            recv_sem=self.recvs.at[sem, slot],
            device_id={self.axis: peer},
            device_id_type=pl.DeviceIdType.MESH,
        )

    def reduces(self, data, land, chunk, slot, b):
        for j in range(self.digits[b] - 1):
            source = data.at[aligned(chunk * self.rows + self.away[b][j], self.size[b + 1])]
            target = land.at[self.landed(chunk, b, j)]
            yield self.remote(source, target, slot, self.sem[b] + j, self.peer[b][j])

    def gathers(self, data, chunk, slot, b):
        here = data.at[self.kept(chunk, b)]
        for j in range(self.digits[b] - 1):
            yield self.remote(here, here, slot, self.copies + self.sem[b] + j, self.peer[b][j])

    def stage(self, s, chunk, slot, data, land, result, finish):
        levels = self.levels
        if 0 < s <= levels:
            b = s - 1
            for copy in self.reduces(data, land, chunk, slot, b):
                copy.wait()
            kept = self.kept(chunk, b)
            total = data[kept, :]
            for j in range(self.digits[b] - 1):
                total += land[self.landed(chunk, b, j), :]
            if s < levels:
                data[kept, :] = total
            else:
                finish(kept, total)
        elif s > levels:
            for copy in self.gathers(result, chunk, slot, 2 * levels - s):
                copy.wait()
        if s < levels:
            for copy in self.reduces(data, land, chunk, slot, s):
                copy.start()
        elif s < 2 * levels:
            for copy in self.gathers(result, chunk, slot, 2 * levels - 1 - s):
                copy.start()


def body(sizes, plane, sens_hbm, obs_hbm, models_hbm, near_ref, mask_ref, out_hbm,
         sens, obs, part, land, weighted, grad, gland, state, high, low, smooth,
         under, over, load_sem, obs_sem, edge_sem, c_send, c_recv, d_send, d_recv, h_send, h_recv):
    n_dp, n_cells = sizes
    ndata, ncell = sens.shape
    halves, _, width = grad.shape
    me = lax.axis_index("cells")
    chunks = c_send.shape[1] // halves
    rows = ndata // chunks
    parts = d_send.shape[1] // halves
    prow = ncell // parts
    per_plane = plane // prow
    dp_digits, cell_digits = radix(n_dp, n_cells)
    cells = Scatter("cells", cell_digits, rows, c_send, c_recv)
    dp = Scatter("dp", dp_digits, prow, d_send, d_recv)
    seg = dp.size[-1]
    own = dp.off[-1]
    units = halves * chunks
    delay = chunks + LAG * cells.stages
    period = delay + parts + DP_LAG * dp.stages
    slots = (ITERS - 1) * period + delay + units - chunks + parts + DP_LAG * dp.stages
    nn, tn = ((1,), (0,)), ((0,), (0,))

    def load(c):
        at = aligned(c * rows, rows)
        return pltpu.make_async_copy(sens_hbm.at[at], sens.at[at], load_sem.at[c])

    def columns(h):
        return pl.ds(h * width, width)

    def enter(h):
        return pltpu.make_async_copy(models_hbm.at[:, columns(h)], state.at[0, h], edge_sem.at[h])

    def leave(h):
        return pltpu.make_async_copy(state.at[ITERS, h], out_hbm.at[:, columns(h)], edge_sem.at[h])

    def watch(h):
        return pltpu.make_async_copy(obs_hbm.at[:, columns(h)], obs.at[h], obs_sem.at[h])

    for h in range(halves):
        enter(h).start()
    for c in range(chunks):
        load(c).start()
    for h in range(halves):
        watch(h).start()

    barrier = pltpu.get_barrier_semaphore()

    def greet(where):
        pl.semaphore_signal(barrier, inc=1, device_id=where, device_id_type=pl.DeviceIdType.MESH)

    for peers in cells.peer:
        for peer in peers:
            greet({"cells": peer})
    for peers in dp.peer:
        for peer in peers:
            greet({"dp": peer})

    has_under, has_over = me > 0, me < n_cells - 1

    @pl.when(has_under)
    def _():
        greet({"cells": me - 1})

    @pl.when(has_over)
    def _():
        greet({"cells": me + 1})

    @pl.when(me == 0)
    def _():
        under[...] = jnp.zeros_like(under)

    @pl.when(me == n_cells - 1)
    def _():
        over[...] = jnp.zeros_like(over)

    for h in range(halves):
        enter(h).wait()

    pl.semaphore_wait(
        barrier,
        cells.copies + dp.copies + (me + n_cells - 1) // n_cells + (2 * n_cells - 2 - me) // n_cells,
    )

    def halo(step, h, i, upward):
        source = (ncell - plane if upward else 0) + i * prow + own
        return pltpu.make_async_remote_copy(
            src_ref=state.at[step, h, aligned(source, seg)],
            dst_ref=(under if upward else over).at[step, h, pl.ds(i * seg, seg)],
            send_sem=h_send.at[step, h, int(upward) * per_plane + i],
            recv_sem=h_recv.at[step, h, int(upward) * per_plane + i],
            device_id={"cells": me + 1 if upward else me - 1},
            device_id_type=pl.DeviceIdType.MESH,
        )

    def halos(act_over, act_under):
        @pl.when(has_over)
        def _():
            for i in range(per_plane):
                act_over(i)

        @pl.when(has_under)
        def _():
            for i in range(per_plane):
                act_under(i)

    def predict(step, h, c):
        @pl.when(c == 0)
        def _():
            halos(
                lambda i: halo(step, h, i, True).start(),
                lambda i: halo(step, h, i, False).start(),
            )
            hi, lo = split(state[step, h])
            high[h] = hi
            low[h] = lo

        @pl.when(jnp.logical_and(step == 0, h == 0))
        def _():
            load(c).wait()

        at = aligned(c * rows, rows)
        s_hi, s_lo = split(sens[at, :])
        part[h, at, :] = dot(s_hi, high[h], nn) + dot(s_hi, low[h], nn) + dot(s_lo, high[h], nn)

    def back(step, h, c):
        @pl.when(c == 0)
        def _():
            grad[h] = jnp.zeros_like(grad[h])

        at = aligned(c * rows, rows)
        s_hi, s_lo = split(sens[at, :])
        w_hi, w_lo = split(weighted[h, at, :])
        grad[h] += dot(s_hi, w_hi, tn) + dot(s_hi, w_lo, tn) + dot(s_lo, w_hi, tn)

    def smooth_part(step, h, q):
        @pl.when(q == 0)
        def _():
            halos(
                lambda i: halo(step, h, i, True).wait_send(),
                lambda i: halo(step, h, i, False).wait_send(),
            )
            halos(
                lambda i: halo(step, h, i, False).wait_recv(),
                lambda i: halo(step, h, i, True).wait_recv(),
            )

        base = q * prow + own
        inner = lax.rem(base, plane)
        first = base - inner
        cell = state[step, h, aligned(base, seg), :]
        total = jnp.zeros_like(cell)

        def add(other):
            diff = other - cell
            return diff / jnp.sqrt(1.0 + diff * diff)

        at = aligned(lax.rem(q, per_plane) * seg, seg)
        below = state[step, h, aligned(jnp.maximum(base - plane, 0), seg), :]
        above = state[step, h, aligned(jnp.minimum(base + plane, ncell - seg), seg), :]
        total += add(jnp.where(first == 0, under[step, h, at, :], below))
        total += add(jnp.where(first == ncell - plane, over[step, h, at, :], above))
        whole = pl.ds(pl.multiple_of(first, 16), plane)
        for k in range(4):
            column = near_ref[aligned(inner, seg), k:k + 1]
            pick = column == lax.broadcasted_iota(jnp.int32, (seg, plane), 1)
            pick = jnp.where(pick, 1.0, 0.0).astype(BF16)
            total += add(dot(pick, high[h, whole, :], nn) + dot(pick, low[h, whole, :], nn))
        scale = 1.0 - 0.75 * mask_ref[aligned(base, seg), :].astype(F32)
        smooth[h, aligned(q * seg, seg), :] = total * scale

    def at_slot(x, count, act):
        step, unit = lax.div(x, period), lax.rem(x, period)
        h, index = lax.div(unit, chunks), lax.rem(unit, chunks)

        @pl.when((x >= 0) & (step < ITERS) & (unit < units) & (index < count))
        def _():
            act(step, h, index)

    def cell_stage(s, step, h, c):
        def reweight(kept, total):
            misfit = total - obs[h, kept, :]
            weighted[h, kept, :] = misfit / jnp.maximum(jnp.abs(misfit), 1.0)

        cells.stage(s, c, h * chunks + c, part.at[h], land.at[h], weighted.at[h], reweight)

    def dp_stage(s, step, h, q):
        def update(kept, total):
            moved = state[step, h, kept, :] - 1.0 * total
            state[step + 1, h, kept, :] = moved + 0.05 * smooth[h, aligned(q * seg, seg), :]

        dp.stage(s, q, h * parts + q, grad.at[h], gland.at[h], state.at[step + 1, h], update)

    def slot(t, carry):
        @pl.when(t == 0)
        def _():
            for h in range(halves):
                watch(h).wait()

        for s in reversed(range(cells.stages + 1)):
            at_slot(t - LAG * s, chunks, functools.partial(cell_stage, s))
        for s in reversed(range(dp.stages + 1)):
            at_slot(t - delay - DP_LAG * s, parts, functools.partial(dp_stage, s))
        at_slot(t + 1, chunks, predict)
        at_slot(t - 2, parts, smooth_part)
        at_slot(t - LAG * cells.stages, chunks, back)
        return carry

    lax.fori_loop(-1, slots, slot, 0)
    for h in range(halves):
        leave(h).start()
    for h in range(halves):
        leave(h).wait()


def invert(n_dp, n_cells, sensitivity, observed, models, neighbour_map, edge_mask):
    ndata, ncell = sensitivity.shape
    width = models.shape[1] // HALVES
    plane = neighbour_map.shape[1]
    rows = max(CHUNK, 8 * n_cells)
    chunks = ndata // rows
    parts = ncell // plane * PARTS
    seg = ncell // parts // n_dp
    vmem = pl.BlockSpec(memory_space=pltpu.VMEM)
    hbm = pl.BlockSpec(memory_space=pl.ANY)
    dma = pltpu.SemaphoreType.DMA
    nd, nb = (2 * sum(d - 1 for d in digits) for digits in radix(n_dp, n_cells))
    return pl.pallas_call(
        functools.partial(body, (n_dp, n_cells), plane),
        out_shape=jax.ShapeDtypeStruct(models.shape, F32),
        in_specs=[hbm] * 3 + [vmem] * 2,
        out_specs=hbm,
        scratch_shapes=[
            pltpu.VMEM((ndata, ncell), F32),
            pltpu.VMEM((HALVES, ndata, width), F32),
            pltpu.VMEM((HALVES, ndata, width), F32),
            pltpu.VMEM((HALVES, ndata, width), F32),
            pltpu.VMEM((HALVES, ndata, width), F32),
            pltpu.VMEM((HALVES, ncell, width), F32),
            pltpu.VMEM((HALVES, ncell, width), F32),
            pltpu.VMEM((ITERS + 1, HALVES, ncell, width), F32),
            pltpu.VMEM((HALVES, ncell, width), BF16),
            pltpu.VMEM((HALVES, ncell, width), BF16),
            pltpu.VMEM((HALVES, parts * seg, width), F32),
            pltpu.VMEM((ITERS, HALVES, PARTS * seg, width), F32),
            pltpu.VMEM((ITERS, HALVES, PARTS * seg, width), F32),
            dma((chunks,)),
            dma((HALVES,)),
            dma((HALVES,)),
            dma((nb, HALVES * chunks)),
            dma((nb, HALVES * chunks)),
            dma((nd, HALVES * parts)),
            dma((nd, HALVES * parts)),
            dma((ITERS, HALVES, 2 * PARTS)),
            dma((ITERS, HALVES, 2 * PARTS)),
        ],
        compiler_params=pltpu.CompilerParams(
            collective_id=0, has_side_effects=True, vmem_limit_bytes=60 * 1024 * 1024
        ),
        name="invert",
    )(sensitivity, observed, models, neighbour_map.T, edge_mask[:, None])


def solution(mesh):
    return jax.shard_map(
        functools.partial(invert, mesh.shape["dp"], mesh.shape["cells"]),
        mesh=mesh,
        in_specs=(P("dp", "cells"), P("dp", None), P("cells", None), P(), P("cells")),
        out_specs=P("cells", None),
        check_vma=False,
    )
```

profile of v0, /device:TPU:0, one launch (start us, length us, event | category | flops | bytes accessed | tf_op | source)
XLA Modules:
  0.0 159.5 jit_solution(4221420902197793169)
XLA Ops:
  0.0 1.6 %copy.7 = s32[4,768]{0,1:T(8,128)} copy(s32[4,768]{1,0:T(4,128)} %param.8) | data formatting | bytes 24576 | tf_op args[3]
  1.6 1.8 %broadcast_in_dim.4.mask_ref = s32[1536,1]{1,0:T(8,128)} reshape(s32[1536]{0:T(1024)} %param.9) | data formatting | bytes 12288 | tf_op jit(solution)/shard_map/broadcast_in_dim | solution.py:381
  3.5 153.3 %invert.1 = f32[1536,256]{1,0:T(8,128)} custom-call(f32[2048,1536]{1,0:T(8,128)} %sens_hbm.1, f32[2048,256]{1,0:T(8,128)} %obs_hbm.1, f32[1536,256]{1,0:T(8,128)} %models_hbm.1, s32[768,4]{1,0:T(8,128)} %bitcast.1, s32[1536,1]{1,0:T(8,128)} %broadcast_in_dim.4.mask_ref), custom_call_target="tpu_custom_call" | custom-call | tf_op jit(solution)/shard_map/invert/pallas_call | solution.py:348
  156.8 2.7 %copy.10 = f32[1536,256]{1,0:T(8,128)} copy(f32[1536,256]{1,0:T(8,128)} %invert.1) | data formatting | bytes 3145728
where the time goes:
time: 160 us; the launch traced here: 159 us
  Pallas kernels  153 us (96%)
  local copies, waits for them, and re-layouts  6.13 us (4%)
    pallas_call x1, Pallas kernels, invert(): pl.pallas_call(functools.partial(body, (n_dp, n_cells), plane), out_shape...  153 us
    unnamed x2, local copies, waits for them, and re-layouts  4.28 us

commit v1 on v0

v1 whole, which is shorter than its diff:
```python
import functools

import jax
import jax.numpy as jnp
from jax import lax
from jax.experimental import pallas as pl
from jax.experimental.pallas import tpu as pltpu
from jax.sharding import PartitionSpec as P

ITERS = 2
CHUNK = 512
GROUPS = 4
CELL_AT = (0, 4, 7, 10, 13, 17)
BACK_LAG = 1
DP_AT = (0, 2, 5, 7)
PIECES = 4
HALO_LAG = 0
HALO_STRIDE = 2
SMOOTH_LAG = 12
STRIDE = 2
TURNED = 0
ORDER = (1, 0)
LANES = 128
F32 = jnp.float32
BF16 = jnp.bfloat16


def split(x):
    hi = x.astype(BF16)
    return hi, (x - hi.astype(F32)).astype(BF16)


def digits_of(count):
    digits = []
    while count > 1:
        digits.append(2)
        count //= 2
    return digits


def dot(a, b, dims):
    return lax.dot_general(a, b, (dims, ((), ())), preferred_element_type=F32)


def over(x, n):
    if n & (n - 1):
        return lax.div(x, n), lax.rem(x, n)
    return lax.shift_right_logical(x, n.bit_length() - 1), lax.bitwise_and(x, n - 1)


def timetable(times, stages):
    times = list(times)
    while len(times) <= stages:
        times.append(times[-1] + 3)
    return times


def lanes(start, size):
    return pl.ds(pl.multiple_of(start, LANES), size)


class Sum:
    def __init__(self, axis, digits, size, cols, sends, recvs, order=(), sem=0):
        strides = [1]
        for base in digits[:-1]:
            strides.append(strides[-1] * base)
        order = list(order) + list(range(len(order), len(digits)))
        self.axis, self.cols, self.pitch = axis, cols, size
        self.sends, self.recvs, self.sem = sends, recvs, sem
        self.last = len(digits) - 1
        self.stages = 2 * self.last + 1
        me = lax.axis_index(axis)
        self.peer, self.away, self.off, self.size = [], [], [0], [size]
        for b in range(len(digits)):
            stride = strides[order[b]]
            mine = (me // stride) % 2
            self.peer.append(me + (1 - 2 * mine) * stride)
            self.mine = mine
            if b < self.last:
                piece = self.size[b] // 2
                self.away.append(self.off[b] + (1 - mine) * piece)
                self.off.append(self.off[b] + mine * piece)
                self.size.append(piece)

    def kept(self, chunk, b):
        return lanes(chunk * self.pitch + self.off[b + 1], self.size[b + 1])

    def landed(self, chunk, b):
        size = self.size[min(b + 1, self.last)]
        return lanes(chunk * self.pitch + self.pitch - self.size[b], size)

    def remote(self, source, target, slot, sem, peer):
        return pltpu.make_async_remote_copy(
            src_ref=source,
            dst_ref=target,
            send_sem=self.sends.at[self.sem + sem, slot],
            recv_sem=self.recvs.at[self.sem + sem, slot],
            device_id={self.axis: peer},
            device_id_type=pl.DeviceIdType.MESH,
        )

    def move(self, s, chunk, slot, data, land, result):
        last = self.last
        if s < last:
            away = lanes(chunk * self.pitch + self.away[s], self.size[s + 1])
            source, target, b = data.at[self.cols, away], land.at[self.cols, self.landed(chunk, s)], s
        elif s == last:
            source, target, b = data.at[self.cols, self.kept(chunk, last - 1)], land.at[self.cols, self.landed(chunk, last)], last
        else:
            b = 2 * last - s
            source = target = result.at[self.cols, self.kept(chunk, b)]
        return self.remote(source, target, slot, s, self.peer[b])

    def stage(self, s, chunk, slot, data, land, result, finish, adjust=None):
        last = self.last
        if s > 0:
            self.move(s - 1, chunk, slot, data, land, result).wait()
        if 0 < s <= last:
            at = self.kept(chunk, s - 1)
            data[self.cols, at] += land[self.cols, self.landed(chunk, s - 1)]
            if s == last and adjust is not None:
                adjust()
        elif s == last + 1:
            at = self.kept(chunk, last - 1)
            finish(self.cols, at, data[self.cols, at] + land[self.cols, self.landed(chunk, last)])
        if s < self.stages:
            self.move(s, chunk, slot, data, land, result).start()


def body(sizes, plane, sens_hbm, obs_hbm, models_hbm, near_ref, mask_ref, out_hbm,
         sens, s_high, s_low, obs_raw, obs, part, land, weighted, grad, gland, flat, state, wide,
         pick, smooth, rim, load_sem, obs_sem, edge_sem, c_send, c_recv, d_send, d_recv, h_send, h_recv):
    n_dp, n_cells = sizes
    ndata, ncell = sens.shape
    groups, width, _ = grad.shape
    per = LANES // width
    me = lax.axis_index("cells")
    chunks = load_sem.shape[0]
    rows = ndata // chunks
    parts = ncell // plane
    prow = ncell // parts
    cell_digits, dp_digits = digits_of(n_cells), digits_of(n_dp)
    straight = width - TURNED
    cells = Sum("cells", cell_digits, rows, pl.ds(0, straight), c_send, c_recv)
    ways = [cells]
    if TURNED:
        order = ORDER if len(cell_digits) >= len(ORDER) else ()
        ways.insert(0, Sum("cells", cell_digits, rows, pl.ds(straight, TURNED), c_send, c_recv, order, cells.stages))
    dp = Sum("dp", dp_digits, prow, pl.ds(0, width), d_send, d_recv)
    seg = dp.size[-1]
    inner = dp.off[-1]
    side = dp.mine
    own = side * prow + inner
    units = groups * chunks
    span = STRIDE * chunks
    cell_at, dp_at = timetable(CELL_AT, cells.stages), timetable(DP_AT, dp.stages)
    behind = cell_at[cells.stages] + BACK_LAG
    delay = span - STRIDE + behind + 1
    done = delay + parts + dp_at[dp.stages]
    period = max(STRIDE * units, done)
    slots = (ITERS - 1) * period + (groups - 1) * span + done
    nn, nt = ((1,), (0,)), ((1,), (1,))

    def load(c):
        at = pl.ds(pl.multiple_of(c * rows, LANES), rows)
        return pltpu.make_async_copy(sens_hbm.at[at], sens.at[at], load_sem.at[c])

    def enter(p):
        at = lanes(p * LANES, LANES)
        return pltpu.make_async_copy(models_hbm.at[:, at], flat.at[:, at], edge_sem.at[p])

    def leave(p):
        at = lanes(p * LANES, LANES)
        return pltpu.make_async_copy(flat.at[:, at], out_hbm.at[:, at], edge_sem.at[p])

    def watch(p):
        at = lanes(p * LANES, LANES)
        return pltpu.make_async_copy(obs_hbm.at[:, at], obs_raw.at[:, at], obs_sem.at[p])

    pairs = groups // per
    for p in range(pairs):
        enter(p).start()
    load(0).start()
    for p in range(pairs):
        watch(p).start()
    for c in range(1, chunks):
        load(c).start()

    barrier = pltpu.get_barrier_semaphore()

    def greet(where):
        pl.semaphore_signal(barrier, inc=1, device_id=where, device_id_type=pl.DeviceIdType.MESH)

    for peer in cells.peer:
        greet({"cells": peer})
    for peer in dp.peer:
        greet({"dp": peer})

    has_under, has_over = me > 0, me < n_cells - 1

    @pl.when(has_under)
    def _():
        greet({"cells": me - 1})

    @pl.when(has_over)
    def _():
        greet({"cells": me + 1})

    upward = side == 0
    gives = (upward & has_over) | (jnp.logical_not(upward) & has_under)
    takes = (upward & has_under) | (jnp.logical_not(upward) & has_over)

    @pl.when(jnp.logical_not(takes))
    def _():
        rim[...] = jnp.zeros_like(rim)

    for p in range(pairs):
        enter(p).wait()
        turned = flat[:, p * LANES:(p + 1) * LANES].T
        for i in range(per):
            state[0, p * per + i] = turned[i * width:(i + 1) * width]

    pl.semaphore_wait(
        barrier,
        len(cell_digits) + len(dp_digits) + (me + n_cells - 1) // n_cells + (2 * n_cells - 2 - me) // n_cells,
    )

    def halo(step, g, i):
        source = (1 - side) * (ncell - plane) + inner
        cols = pl.ds(pl.multiple_of(i * (width // PIECES), 8), width // PIECES)
        return pltpu.make_async_remote_copy(
            src_ref=state.at[step, g, cols, lanes(source, seg)],
            dst_ref=rim.at[step, g, cols],
            send_sem=h_send.at[step, g * PIECES + i],
            recv_sem=h_recv.at[step, g * PIECES + i],
            device_id={"cells": me + 1 - 2 * side},
            device_id_type=pl.DeviceIdType.MESH,
        )

    def border(step, g, i):
        @pl.when(gives)
        def _():
            halo(step, g, i).start()

    def predict(step, g, c):
        @pl.when(c == 0)
        def _():
            hi, lo = split(state[step, g])
            wide[g, :width, :] = hi
            wide[g, width:, :] = lo

        at = pl.ds(pl.multiple_of(c * rows, LANES), rows)

        @pl.when((step == 0) & (g == 0))
        def _():
            load(c).wait()
            hi, lo = split(sens[at, :])
            s_high[at, :] = hi
            s_low[at, :] = lo

        both = dot(wide[g], s_high[at, :], nt)
        part[g, :, at] = both[:width] + both[width:] + dot(wide[g, :width, :], s_low[at, :], nt)

    def sight(step, g, c):
        @pl.when((step == 0) & (lax.rem(g, per) == 0))
        def _():
            p = lax.div(g, per)

            @pl.when(c == 0)
            def _():
                watch(p).wait()

            at = lanes(c * rows, rows)
            turned = obs_raw[at, lanes(p * LANES, LANES)].T
            for i in range(per):
                obs[g + i, :, at] = turned[i * width:(i + 1) * width]

    def back(step, g, c):
        @pl.when(c == 0)
        def _():
            grad[g] = jnp.zeros_like(grad[g])

        at = pl.ds(pl.multiple_of(c * rows, LANES), rows)
        hi, lo = split(weighted[g, :, at])
        both = dot(jnp.concatenate([hi, lo], axis=0), s_high[at, :], nn)
        grad[g] += both[:width] + both[width:] + dot(hi, s_low[at, :], nn)

    def smooth_part(step, g, k):
        @pl.when((step == 0) & (g == 0))
        def _():
            row = near_ref[pl.ds(k, 1), lanes(inner, seg)]
            chosen = lax.broadcasted_iota(jnp.int32, (plane, seg), 0) == row
            pick[k] = jnp.where(chosen, 1.0, 0.0).astype(BF16)

        cell = state[step, g, :, lanes(own, seg)]

        def pull(other):
            diff = other - cell
            return diff / jnp.sqrt(1.0 + diff * diff)

        @pl.when(k == 0)
        def _():
            @pl.when(gives)
            def _():
                for i in range(PIECES):
                    halo(step, g, i).wait_send()

            @pl.when(takes)
            def _():
                for i in range(PIECES):
                    halo(step, g, i).wait_recv()

            beside = state[step, g, :, lanes((1 - side) * prow + inner, seg)]
            smooth[g] = pull(rim[step, g]) + pull(beside)

        both = dot(wide[g, :, lanes(side * plane, plane)], pick[k], nn)
        scale = jnp.where(k == 3, 0.05, 1.0) * jnp.where(k == 3, 1.0 - 0.75 * mask_ref[:, lanes(own, seg)].astype(F32), 1.0)
        smooth[g] = (smooth[g] + pull(both[:width] + both[width:])) * scale

    def at_slot(x, count, stride, act):
        step = sum((x >= i * period).astype(jnp.int32) for i in range(1, ITERS))
        g, place = over(x - step * period, span)
        index, wait = over(place, stride)

        @pl.when((x >= 0) & (g < groups) & (index < count) & (wait == 0))
        def _():
            act(step, g, index)

    def cell_stage(s, step, g, c):
        def reweight(cols, at, total):
            misfit = total - obs[g, cols, at]
            weighted[g, cols, at] = misfit / jnp.maximum(jnp.abs(misfit), 1.0)

        for way in ways:
            way.stage(s, c, step * units + g * chunks + c, part.at[g], land.at[step, g], weighted.at[g], reweight)

    def dp_stage(s, step, g, q):
        def blend():
            @pl.when(side == q)
            def _():
                grad[g, :, lanes(own, seg)] -= smooth[g]

        def update(cols, at, total):
            state[step + 1, g, :, at] = state[step, g, :, at] - 1.0 * total

        slot = (step * groups + g) * parts + q
        dp.stage(s, q, slot, grad.at[g], gland.at[step, g], state.at[step + 1, g], update, blend)

    def depart(step, g, i):
        @pl.when((step == ITERS - 1) & (lax.rem(g, per) == per - 1))
        def _():
            p = lax.div(g, per)
            rest = [state[ITERS, g - per + 1 + i] for i in range(per)]
            flat[:, lanes(p * LANES, LANES)] = jnp.concatenate(rest, axis=0).T
            leave(p).start()

    def slot(t, carry):
        for s in reversed(range(cells.stages + 1)):
            at_slot(t - cell_at[s], chunks, STRIDE, functools.partial(cell_stage, s))
        for s in reversed(range(dp.stages + 1)):
            at_slot(t - delay - dp_at[s], parts, 1, functools.partial(dp_stage, s))
        at_slot(t + 1, chunks, STRIDE, predict)
        at_slot(t - HALO_LAG, PIECES, HALO_STRIDE, border)
        at_slot(t, chunks, STRIDE, sight)
        at_slot(t - SMOOTH_LAG, 4, 1, smooth_part)
        at_slot(t - behind, chunks, STRIDE, back)
        at_slot(t - done + 1, 1, 1, depart)
        return carry

    lax.fori_loop(-1, slots, slot, 0)
    for p in range(pairs):
        leave(p).wait()


def invert(n_dp, n_cells, sensitivity, observed, models, neighbour_map, edge_mask):
    ndata, ncell = sensitivity.shape
    total = models.shape[1]
    width = total // GROUPS
    plane = neighbour_map.shape[1]
    nb, nd = 2 * len(digits_of(n_cells)) - 1, 2 * len(digits_of(n_dp)) - 1
    chunks = ndata // max(CHUNK, LANES * n_cells // 2)
    parts = ncell // plane
    seg = ncell // n_dp
    ways = 2 if TURNED else 1
    vmem = pl.BlockSpec(memory_space=pltpu.VMEM)
    hbm = pl.BlockSpec(memory_space=pl.ANY)
    dma = pltpu.SemaphoreType.DMA
    return pl.pallas_call(
        functools.partial(body, (n_dp, n_cells), plane),
        out_shape=jax.ShapeDtypeStruct(models.shape, F32),
        in_specs=[hbm] * 3 + [vmem] * 2,
        out_specs=hbm,
        scratch_shapes=[
            pltpu.VMEM((ndata, ncell), F32),
            pltpu.VMEM((ndata, ncell), BF16),
            pltpu.VMEM((ndata, ncell), BF16),
            pltpu.VMEM((ndata, total), F32),
            pltpu.VMEM((GROUPS, width, ndata), F32),
            pltpu.VMEM((GROUPS, width, ndata), F32),
            pltpu.VMEM((ITERS, GROUPS, width, ndata), F32),
            pltpu.VMEM((GROUPS, width, ndata), F32),
            pltpu.VMEM((GROUPS, width, ncell), F32),
            pltpu.VMEM((ITERS, GROUPS, width, ncell), F32),
            pltpu.VMEM((ncell, total), F32),
            pltpu.VMEM((ITERS + 1, GROUPS, width, ncell), F32),
            pltpu.VMEM((GROUPS, 2 * width, ncell), BF16),
            pltpu.VMEM((4, plane, seg), BF16),
            pltpu.VMEM((GROUPS, width, seg), F32),
            pltpu.VMEM((ITERS, GROUPS, width, seg), F32),
            dma((chunks,)),
            dma((GROUPS * width // LANES,)),
            dma((GROUPS * width // LANES,)),
            dma((ways * nb, ITERS * GROUPS * chunks)),
            dma((ways * nb, ITERS * GROUPS * chunks)),
            dma((nd, ITERS * GROUPS * parts)),
            dma((nd, ITERS * GROUPS * parts)),
            dma((ITERS, GROUPS * PIECES)),
            dma((ITERS, GROUPS * PIECES)),
        ],
        compiler_params=pltpu.CompilerParams(
            collective_id=0, has_side_effects=True, vmem_limit_bytes=63 * 1024 * 1024
        ),
        name="invert",
    )(sensitivity, observed, models, neighbour_map, edge_mask[None, :])


def solution(mesh):
    return jax.shard_map(
        functools.partial(invert, mesh.shape["dp"], mesh.shape["cells"]),
        mesh=mesh,
        in_specs=(P("dp", "cells"), P("dp", None), P("cells", None), P(), P("cells")),
        out_specs=P("cells", None),
        check_vma=False,
    )
```

time: 160 us -> 147 us (0.919)
  Pallas kernels: 153 us -> 142 us
  local copies, waits for them, and re-layouts: 6.13 us -> 3.95 us
    pallas_call x1, Pallas kernels: 153 us -> 142 us  [invert(): pl.pallas_call(functools.partial(body, (n_dp, n_cells), plane), out_shape...]
    unnamed x2 -> x1, local copies, waits for them, and re-layouts: 4.28 us -> 2.65 us
where the time goes in v1:
time: 147 us; the launch traced here: 146 us
  Pallas kernels  142 us (97%)
  local copies, waits for them, and re-layouts  3.95 us (3%)
    pallas_call x1, Pallas kernels, invert(): pl.pallas_call(functools.partial(body, (n_dp, n_cells), plane), out_shape...  142 us

profile of v1, /device:TPU:0, one launch (start us, length us, event | category | flops | bytes accessed | tf_op | source)
XLA Modules:
  0.0 146.4 jit_solution(3860220864726387243)
XLA Ops:
  0.0 1.3 broadcast_in_dim.3.mask_ref
  1.3 142.4 %invert.1 = f32[1536,256]{1,0:T(8,128)} custom-call(f32[2048,1536]{1,0:T(8,128)} %sens_hbm.1, f32[2048,256]{1,0:T(8,128)} %obs_hbm.1, f32[1536,256]{1,0:T(8,128)} %models_hbm.1, s32[4,768]{1,0:T(4,128)} %near_ref.1, s32[1,1536]{1,0:T(1,128)} %broadcast_in_dim.3.mask_ref), custom_call_target="tpu_custom_call" | custom-call | tf_op jit(solution)/shard_map/invert/pallas_call | solution.py:388
  143.7 2.7 %copy.7 = f32[1536,256]{1,0:T(8,128)} copy(f32[1536,256]{1,0:T(8,128)} %invert.1) | data formatting | bytes 3145728

commit v2 on v1

--- a/solution.py
+++ b/solution.py
@@ -10,7 +10,7 @@
 ITERS = 2
 CHUNK = 512
 GROUPS = 4
-CELL_AT = (0, 4, 7, 10, 13, 17)
+CELL_AT = (0, 3, 6, 9, 12, 15)
 BACK_LAG = 1
 DP_AT = (0, 2, 5, 7)
 PIECES = 4
@@ -18,8 +18,7 @@
 HALO_STRIDE = 2
 SMOOTH_LAG = 12
 STRIDE = 2
-TURNED = 0
-ORDER = (1, 0)
+TURNED = 32
 LANES = 128
 F32 = jnp.float32
 BF16 = jnp.bfloat16
@@ -60,19 +59,18 @@
 
 
 class Sum:
-    def __init__(self, axis, digits, size, cols, sends, recvs, order=(), sem=0):
+    def __init__(self, axis, digits, size, cols, sends, recvs):
         strides = [1]
         for base in digits[:-1]:
             strides.append(strides[-1] * base)
-        order = list(order) + list(range(len(order), len(digits)))
         self.axis, self.cols, self.pitch = axis, cols, size
-        self.sends, self.recvs, self.sem = sends, recvs, sem
+        self.sends, self.recvs = sends, recvs
         self.last = len(digits) - 1
         self.stages = 2 * self.last + 1
         me = lax.axis_index(axis)
         self.peer, self.away, self.off, self.size = [], [], [0], [size]
         for b in range(len(digits)):
-            stride = strides[order[b]]
+            stride = strides[b]
             mine = (me // stride) % 2
             self.peer.append(me + (1 - 2 * mine) * stride)
             self.mine = mine
@@ -93,8 +91,8 @@
         return pltpu.make_async_remote_copy(
             src_ref=source,
             dst_ref=target,
-            send_sem=self.sends.at[self.sem + sem, slot],
-            recv_sem=self.recvs.at[self.sem + sem, slot],
+            send_sem=self.sends.at[sem, slot],
+            recv_sem=self.recvs.at[sem, slot],
             device_id={self.axis: peer},
             device_id_type=pl.DeviceIdType.MESH,
         )
@@ -127,6 +125,147 @@
             self.move(s, chunk, slot, data, land, result).start()
 
 
+class Move:
+    def __init__(self, **names):
+        self.names = names
+
+    def start(self):
+        pltpu.make_async_remote_copy(**self.names).start()
+
+    def wait(self):
+        pltpu.make_async_remote_copy(**self.names).wait()
+
+    def wait_send(self):
+        pltpu.make_async_remote_copy(**self.names).wait_send()
+
+    def wait_recv(self):
+        pltpu.make_async_remote_copy(**self.names).wait_recv()
+
+
+class Ladder:
+    def __init__(self, across, size, cols, sends, recvs, sem):
+        self.size, self.half, self.cols, self.across = size, size // 2, cols, across
+        self.sends, self.recvs, self.sem = sends, recvs, sem
+        self.stages = 5
+        me = lax.axis_index("cells")
+        z, x = me // 2, me % 2
+        self.inner = (z == 1) | (z == 2)
+        self.side, self.rank = x, z // 2
+        self.beside = me + 1 - 2 * x
+        self.mate = me + 2 - 4 * (z % 2)
+        self.other = me + 2 - 4 * (z // 2)
+
+    def lane(self, chunk, start, size):
+        return lanes(chunk * self.size + start, size)
+
+    def spot(self, chunk, start, size):
+        return lanes(chunk * 2 * self.size + start, size)
+
+    def copy(self, source, target, slot, sem, peer):
+        return Move(
+            src_ref=source,
+            dst_ref=target,
+            send_sem=self.sends.at[self.sem + sem, slot],
+            recv_sem=self.recvs.at[self.sem + sem, slot],
+            device_id={"cells": peer},
+            device_id_type=pl.DeviceIdType.MESH,
+        )
+
+    def stage(self, s, chunk, slot, data, land, result, finish):
+        (self.stage_across if self.across else self.stage_along)(s, chunk, slot, data, land, result, finish)
+
+    def stage_across(self, s, chunk, slot, data, land, result, finish):
+        cols, half = self.cols, self.half
+        mine = self.lane(chunk, self.side * half, half)
+        away = self.lane(chunk, (1 - self.side) * half, half)
+        spots = [self.spot(chunk, i * half, half) for i in range(3)]
+        first = self.copy(data.at[cols, away], land.at[cols, spots[0]], slot, 0, self.beside)
+        up = self.copy(data.at[cols, mine], land.at[cols, spots[1]], slot, 1, self.mate)
+        swap = self.copy(data.at[cols, mine], land.at[cols, spots[2]], slot, 2, self.other)
+        down = self.copy(result.at[cols, mine], result.at[cols, mine], slot, 3, self.mate)
+        last = self.copy(result.at[cols, mine], result.at[cols, mine], slot, 4, self.beside)
+        inner, outer = pl.when(self.inner), pl.when(jnp.logical_not(self.inner))
+        if s == 0:
+            first.start()
+        elif s == 1:
+            first.wait()
+            data[cols, mine] += land[cols, spots[0]]
+            outer(up.start)
+        elif s == 2:
+            outer(up.wait_send)
+
+            @inner
+            def _():
+                up.wait_recv()
+                data[cols, mine] += land[cols, spots[1]]
+                swap.start()
+        elif s == 3:
+            @inner
+            def _():
+                swap.wait()
+                finish(cols, mine, data[cols, mine] + land[cols, spots[2]])
+                down.start()
+                last.start()
+        elif s == 4:
+            inner(down.wait_send)
+
+            @outer
+            def _():
+                down.wait_recv()
+                last.start()
+        else:
+            last.wait()
+
+    def stage_along(self, s, chunk, slot, data, land, result, finish):
+        cols, half, size = self.cols, self.half, self.size
+        whole = self.lane(chunk, 0, size)
+        mine = self.lane(chunk, self.rank * half, half)
+        away = self.lane(chunk, (1 - self.rank) * half, half)
+        begin = self.spot(chunk, 0, size)
+        spots = [self.spot(chunk, size + i * half, half) for i in range(2)]
+        up = self.copy(data.at[cols, whole], land.at[cols, begin], slot, 0, self.mate)
+        first = self.copy(data.at[cols, away], land.at[cols, spots[0]], slot, 1, self.other)
+        swap = self.copy(data.at[cols, mine], land.at[cols, spots[1]], slot, 2, self.beside)
+        last = self.copy(result.at[cols, mine], result.at[cols, mine], slot, 3, self.other)
+        near = self.copy(result.at[cols, mine], result.at[cols, mine], slot, 4, self.mate)
+        far = self.copy(result.at[cols, away], result.at[cols, away], slot, 5, self.mate)
+        inner, outer = pl.when(self.inner), pl.when(jnp.logical_not(self.inner))
+        if s == 0:
+            outer(up.start)
+        elif s == 1:
+            outer(up.wait_send)
+
+            @inner
+            def _():
+                up.wait_recv()
+                data[cols, whole] += land[cols, begin]
+                first.start()
+        elif s == 2:
+            @inner
+            def _():
+                first.wait()
+                data[cols, mine] += land[cols, spots[0]]
+                swap.start()
+        elif s == 3:
+            @inner
+            def _():
+                swap.wait()
+                finish(cols, mine, data[cols, mine] + land[cols, spots[1]])
+                last.start()
+                near.start()
+        elif s == 4:
+            inner(near.wait_send)
+            outer(near.wait_recv)
+
+            @inner
+            def _():
+                last.wait()
+                far.start()
+        else:
+            inner(far.wait_send)
+            outer(far.wait_recv)
+
+
 def body(sizes, plane, sens_hbm, obs_hbm, models_hbm, near_ref, mask_ref, out_hbm,
          sens, s_high, s_low, obs_raw, obs, part, land, weighted, grad, gland, flat, state, wide,
          pick, smooth, rim, load_sem, obs_sem, edge_sem, c_send, c_recv, d_send, d_recv, h_send, h_recv):
@@ -140,12 +279,15 @@
     parts = ncell // plane
     prow = ncell // parts
     cell_digits, dp_digits = digits_of(n_cells), digits_of(n_dp)
-    straight = width - TURNED
-    cells = Sum("cells", cell_digits, rows, pl.ds(0, straight), c_send, c_recv)
-    ways = [cells]
-    if TURNED:
-        order = ORDER if len(cell_digits) >= len(ORDER) else ()
-        ways.insert(0, Sum("cells", cell_digits, rows, pl.ds(straight, TURNED), c_send, c_recv, order, cells.stages))
+    if len(cell_digits) == 3:
+        straight = width - TURNED
+        ways = [
+            Ladder(False, rows, pl.ds(straight, TURNED), c_send, c_recv, 5),
+            Ladder(True, rows, pl.ds(0, straight), c_send, c_recv, 0),
+        ]
+    else:
+        ways = [Sum("cells", cell_digits, rows, pl.ds(0, width), c_send, c_recv)]
+    cells = ways[0]
     dp = Sum("dp", dp_digits, prow, pl.ds(0, width), d_send, d_recv)
     seg = dp.size[-1]
     inner = dp.off[-1]
@@ -191,20 +333,12 @@
     def greet(where):
         pl.semaphore_signal(barrier, inc=1, device_id=where, device_id_type=pl.DeviceIdType.MESH)
 
-    for peer in cells.peer:
-        greet({"cells": peer})
+    for d in range(1, n_cells):
+        greet({"cells": lax.rem(me + d, n_cells)})
     for peer in dp.peer:
         greet({"dp": peer})
 
     has_under, has_over = me > 0, me < n_cells - 1
-
-    @pl.when(has_under)
-    def _():
-        greet({"cells": me - 1})
-
-    @pl.when(has_over)
-    def _():
-        greet({"cells": me + 1})
 
     upward = side == 0
     gives = (upward & has_over) | (jnp.logical_not(upward) & has_under)
@@ -220,10 +354,7 @@
         for i in range(per):
             state[0, p * per + i] = turned[i * width:(i + 1) * width]
 
-    pl.semaphore_wait(
-        barrier,
-        len(cell_digits) + len(dp_digits) + (me + n_cells - 1) // n_cells + (2 * n_cells - 2 - me) // n_cells,
-    )
+    pl.semaphore_wait(barrier, n_cells - 1 + len(dp_digits))
 
     def halo(step, g, i):
         source = (1 - side) * (ncell - plane) + inner
@@ -381,7 +512,7 @@
     chunks = ndata // max(CHUNK, LANES * n_cells // 2)
     parts = ncell // plane
     seg = ncell // n_dp
-    ways = 2 if TURNED else 1
+    copies = 11 if n_cells == 8 else nb
     vmem = pl.BlockSpec(memory_space=pltpu.VMEM)
     hbm = pl.BlockSpec(memory_space=pl.ANY)
     dma = pltpu.SemaphoreType.DMA
@@ -397,7 +528,7 @@
             pltpu.VMEM((ndata, total), F32),
             pltpu.VMEM((GROUPS, width, ndata), F32),
             pltpu.VMEM((GROUPS, width, ndata), F32),
-            pltpu.VMEM((ITERS, GROUPS, width, ndata), F32),
+            pltpu.VMEM((ITERS, GROUPS, width, 2 * ndata), F32),
             pltpu.VMEM((GROUPS, width, ndata), F32),
             pltpu.VMEM((GROUPS, width, ncell), F32),
             pltpu.VMEM((ITERS, GROUPS, width, ncell), F32),
@@ -410,8 +541,8 @@
             dma((chunks,)),
             dma((GROUPS * width // LANES,)),
             dma((GROUPS * width // LANES,)),
-            dma((ways * nb, ITERS * GROUPS * chunks)),
-            dma((ways * nb, ITERS * GROUPS * chunks)),
+            dma((copies, ITERS * GROUPS * chunks)),
+            dma((copies, ITERS * GROUPS * chunks)),
             dma((nd, ITERS * GROUPS * parts)),
             dma((nd, ITERS * GROUPS * parts)),
             dma((ITERS, GROUPS * PIECES)),

time: 147 us -> 139 us (0.946)
  Pallas kernels: 142 us -> 135 us
    pallas_call x1, Pallas kernels: 142 us -> 135 us  [invert(): pl.pallas_call(functools.partial(body, (n_dp, n_cells), plane), out_shape...]
where the time goes in v2:
time: 139 us
  Pallas kernels  135 us (97%)
  local copies, waits for them, and re-layouts  3.95 us (3%)
    pallas_call x1, Pallas kernels, invert(): pl.pallas_call(functools.partial(body, (n_dp, n_cells), plane), out_shape...  135 us

profile of v2, /device:TPU:0, one launch (start us, length us, event | category | flops | bytes accessed | tf_op | source)
XLA Modules:
  0.0 138.7 jit_solution(16241212283814416469)
XLA Ops:
  0.0 1.3 broadcast_in_dim.3.mask_ref
  1.3 134.7 %invert.1 = f32[1536,256]{1,0:T(8,128)} custom-call(f32[2048,1536]{1,0:T(8,128)} %sens_hbm.1, f32[2048,256]{1,0:T(8,128)} %obs_hbm.1, f32[1536,256]{1,0:T(8,128)} %models_hbm.1, s32[4,768]{1,0:T(4,128)} %near_ref.1, s32[1,1536]{1,0:T(1,128)} %broadcast_in_dim.3.mask_ref), custom_call_target="tpu_custom_call" | custom-call | tf_op jit(solution)/shard_map/invert/pallas_call | solution.py:519
  136.0 2.7 %copy.7 = f32[1536,256]{1,0:T(8,128)} copy(f32[1536,256]{1,0:T(8,128)} %invert.1) | data formatting | bytes 3145728

commit v3 on v2

--- a/solution.py
+++ b/solution.py
@@ -9,6 +9,8 @@
 
 ITERS = 2
 CHUNK = 512
+LOAD = 256
+TURN_LAG = 0
 GROUPS = 4
 CELL_AT = (0, 3, 6, 9, 12, 15)
 BACK_LAG = 1
@@ -16,7 +18,7 @@
 PIECES = 4
 HALO_LAG = 0
 HALO_STRIDE = 2
-SMOOTH_LAG = 12
+SMOOTH_LAG = 11
 STRIDE = 2
 TURNED = 32
 LANES = 128
@@ -267,14 +269,16 @@
 
 
 def body(sizes, plane, sens_hbm, obs_hbm, models_hbm, near_ref, mask_ref, out_hbm,
-         sens, s_high, s_low, obs_raw, obs, part, land, weighted, grad, gland, flat, state, wide,
+         sens, s_high, s_low, t_high, t_low, obs_raw, obs, part, land, weighted, grad, gland, flat, state, wide,
          pick, smooth, rim, load_sem, obs_sem, edge_sem, c_send, c_recv, d_send, d_recv, h_send, h_recv):
     n_dp, n_cells = sizes
-    ndata, ncell = sens.shape
+    ndata, ncell = s_high.shape
     groups, width, _ = grad.shape
     per = LANES // width
     me = lax.axis_index("cells")
-    chunks = load_sem.shape[0]
+    chunks = c_send.shape[1] // (ITERS * groups)
+    loads = load_sem.shape[0]
+    batch = ndata // loads
     rows = ndata // chunks
     parts = ncell // plane
     prow = ncell // parts
@@ -304,8 +308,8 @@
     nn, nt = ((1,), (0,)), ((1,), (1,))
 
     def load(c):
-        at = pl.ds(pl.multiple_of(c * rows, LANES), rows)
-        return pltpu.make_async_copy(sens_hbm.at[at], sens.at[at], load_sem.at[c])
+        at = pl.ds(pl.multiple_of(c * batch, LANES), batch)
+        return pltpu.make_async_copy(sens_hbm.at[at], sens.at[lax.rem(c, 2)], load_sem.at[c])
 
     def enter(p):
         at = lanes(p * LANES, LANES)
@@ -325,7 +329,7 @@
     load(0).start()
     for p in range(pairs):
         watch(p).start()
-    for c in range(1, chunks):
+    for c in range(1, min(2, loads)):
         load(c).start()
 
     barrier = pltpu.get_barrier_semaphore()
@@ -374,23 +378,58 @@
             halo(step, g, i).start()
 
     def predict(step, g, c):
-        @pl.when(c == 0)
+        p, i = over(g, per)
+        at = pl.ds(pl.multiple_of(c * rows, LANES), rows)
+        joint = (step == 0) & (i == 0)
+        top = pl.ds(pl.multiple_of(i * width, 16), width)
+        low = pl.ds(pl.multiple_of(LANES + i * width, 16), width)
+
+        @pl.when((c == 0) & joint)
+        def _():
+            for n in range(per):
+                hi, lo = split(state[0, g + n])
+                wide[p, n * width:(n + 1) * width, :] = hi
+                wide[p, LANES + n * width:LANES + (n + 1) * width, :] = lo
+
+        @pl.when((c == 0) & (step > 0))
         def _():
             hi, lo = split(state[step, g])
-            wide[g, :width, :] = hi
-            wide[g, width:, :] = lo
-
-        at = pl.ds(pl.multiple_of(c * rows, LANES), rows)
+            wide[p, top, :] = hi
+            wide[p, low, :] = lo
 
         @pl.when((step == 0) & (g == 0))
         def _():
-            load(c).wait()
-            hi, lo = split(sens[at, :])
-            s_high[at, :] = hi
-            s_low[at, :] = lo
-
-        both = dot(wide[g], s_high[at, :], nt)
-        part[g, :, at] = both[:width] + both[width:] + dot(wide[g, :width, :], s_low[at, :], nt)
+            for n in range(rows // batch):
+                b = c * (rows // batch) + n
+                load(b).wait()
+                into = pl.ds(pl.multiple_of(b * batch, LANES), batch)
+                hi, lo = split(sens[lax.rem(b, 2)])
+                s_high[into, :] = hi
+                s_low[into, :] = lo
+
+                @pl.when(b + 2 < loads)
+                def _():
+                    load(b + 2).start()
+
+        @pl.when(joint)
+        def _():
+            both = dot(wide[p], s_high[at, :], nt)
+            total = both[:LANES] + both[LANES:] + dot(wide[p, :LANES, :], s_low[at, :], nt)
+            for n in range(per):
+                part[g + n, :, at] = total[n * width:(n + 1) * width]
+
+        @pl.when(step > 0)
+        def _():
+            hi = wide[p, top, :]
+            both = dot(jnp.concatenate([hi, wide[p, low, :]], axis=0), t_high[:, at], nn)
+            part[g, :, at] = both[:width] + both[width:] + dot(hi, t_low[:, at], nn)
+
+    def turn(step, g, c):
+        @pl.when((step == 0) & (g == 1))
+        def _():
+            at = pl.ds(pl.multiple_of(c * rows, LANES), rows)
+            t_high[:, at] = s_high[at, :].T
+            t_low[:, at] = s_low[at, :].T
 
     def sight(step, g, c):
         @pl.when((step == 0) & (lax.rem(g, per) == 0))
@@ -417,13 +456,21 @@
         grad[g] += both[:width] + both[width:] + dot(hi, s_low[at, :], nn)
 
     def smooth_part(step, g, k):
-        @pl.when((step == 0) & (g == 0))
+        p, i = over(g, per)
+
+        @pl.when(i == per - 1)
+        def _():
+            smooth_pair(step, p, k)
+
+    def smooth_pair(step, p, k):
+        @pl.when((step == 0) & (p == 0))
         def _():
             row = near_ref[pl.ds(k, 1), lanes(inner, seg)]
             chosen = lax.broadcasted_iota(jnp.int32, (plane, seg), 0) == row
             pick[k] = jnp.where(chosen, 1.0, 0.0).astype(BF16)
 
-        cell = state[step, g, :, lanes(own, seg)]
+        mine = pl.ds(p * per, per)
+        cell = state[step, mine, :, lanes(own, seg)]
 
         def pull(other):
             diff = other - cell
@@ -433,20 +480,23 @@
         def _():
             @pl.when(gives)
             def _():
-                for i in range(PIECES):
-                    halo(step, g, i).wait_send()
+                for n in range(per):
+                    for i in range(PIECES):
+                        halo(step, p * per + n, i).wait_send()
 
             @pl.when(takes)
             def _():
-                for i in range(PIECES):
-                    halo(step, g, i).wait_recv()
-
-            beside = state[step, g, :, lanes((1 - side) * prow + inner, seg)]
-            smooth[g] = pull(rim[step, g]) + pull(beside)
-
-        both = dot(wide[g, :, lanes(side * plane, plane)], pick[k], nn)
-        scale = jnp.where(k == 3, 0.05, 1.0) * jnp.where(k == 3, 1.0 - 0.75 * mask_ref[:, lanes(own, seg)].astype(F32), 1.0)
-        smooth[g] = (smooth[g] + pull(both[:width] + both[width:])) * scale
+                for n in range(per):
+                    for i in range(PIECES):
+                        halo(step, p * per + n, i).wait_recv()
+
+            beside = state[step, mine, :, lanes((1 - side) * prow + inner, seg)]
+            smooth[mine] = pull(rim[step, mine]) + pull(beside)
+
+        both = dot(wide[p, :, lanes(side * plane, plane)], pick[k], nn)
+        other = (both[:LANES] + both[LANES:]).reshape(per, width, seg)
+        scale = jnp.where(k == 3, 0.05 * (1.0 - 0.75 * mask_ref[:, lanes(own, seg)].astype(F32)), 1.0)
+        smooth[mine] = (smooth[mine] + pull(other)) * scale
 
     def at_slot(x, count, stride, act):
         step = sum((x >= i * period).astype(jnp.int32) for i in range(1, ITERS))
@@ -493,6 +543,7 @@
         at_slot(t + 1, chunks, STRIDE, predict)
         at_slot(t - HALO_LAG, PIECES, HALO_STRIDE, border)
         at_slot(t, chunks, STRIDE, sight)
+        at_slot(t + 1 - TURN_LAG, chunks, STRIDE, turn)
         at_slot(t - SMOOTH_LAG, 4, 1, smooth_part)
         at_slot(t - behind, chunks, STRIDE, back)
         at_slot(t - done + 1, 1, 1, depart)
@@ -522,9 +573,11 @@
         in_specs=[hbm] * 3 + [vmem] * 2,
         out_specs=hbm,
         scratch_shapes=[
-            pltpu.VMEM((ndata, ncell), F32),
+            pltpu.VMEM((2, LOAD, ncell), F32),
             pltpu.VMEM((ndata, ncell), BF16),
             pltpu.VMEM((ndata, ncell), BF16),
+            pltpu.VMEM((ncell, ndata), BF16),
+            pltpu.VMEM((ncell, ndata), BF16),
             pltpu.VMEM((ndata, total), F32),
             pltpu.VMEM((GROUPS, width, ndata), F32),
             pltpu.VMEM((GROUPS, width, ndata), F32),
@@ -534,11 +587,11 @@
             pltpu.VMEM((ITERS, GROUPS, width, ncell), F32),
             pltpu.VMEM((ncell, total), F32),
             pltpu.VMEM((ITERS + 1, GROUPS, width, ncell), F32),
-            pltpu.VMEM((GROUPS, 2 * width, ncell), BF16),
+            pltpu.VMEM((GROUPS * width // LANES, 2 * LANES, ncell), BF16),
             pltpu.VMEM((4, plane, seg), BF16),
             pltpu.VMEM((GROUPS, width, seg), F32),
             pltpu.VMEM((ITERS, GROUPS, width, seg), F32),
-            dma((chunks,)),
+            dma((ndata // LOAD,)),
             dma((GROUPS * width // LANES,)),
             dma((GROUPS * width // LANES,)),
             dma((copies, ITERS * GROUPS * chunks)),
@@ -549,7 +602,7 @@
             dma((ITERS, GROUPS * PIECES)),
         ],
         compiler_params=pltpu.CompilerParams(
-            collective_id=0, has_side_effects=True, vmem_limit_bytes=63 * 1024 * 1024
+            collective_id=0, has_side_effects=True, vmem_limit_bytes=67043328
         ),
         name="invert",
     )(sensitivity, observed, models, neighbour_map, edge_mask[None, :])

time: 139 us -> 133 us (0.957)
  Pallas kernels: 135 us -> 129 us
    pallas_call x1, Pallas kernels: 135 us -> 129 us  [invert(): pl.pallas_call(functools.partial(body, (n_dp, n_cells), plane), out_shape...]
where the time goes in v3:
time: 133 us
  Pallas kernels  129 us (97%)
  local copies, waits for them, and re-layouts  3.95 us (3%)
    pallas_call x1, Pallas kernels, invert(): pl.pallas_call(functools.partial(body, (n_dp, n_cells), plane), out_shape...  129 us

profile of v3, /device:TPU:0, one launch (start us, length us, event | category | flops | bytes accessed | tf_op | source)
XLA Modules:
  0.0 132.6 jit_solution(1050422674820139864)
XLA Ops:
  0.0 1.3 broadcast_in_dim.3.mask_ref
  1.3 128.6 %invert.1 = f32[1536,256]{1,0:T(8,128)} custom-call(f32[2048,1536]{1,0:T(8,128)} %sens_hbm.1, f32[2048,256]{1,0:T(8,128)} %obs_hbm.1, f32[1536,256]{1,0:T(8,128)} %models_hbm.1, s32[4,768]{1,0:T(4,128)} %near_ref.1, s32[1,1536]{1,0:T(1,128)} %broadcast_in_dim.3.mask_ref), custom_call_target="tpu_custom_call" | custom-call | tf_op jit(solution)/shard_map/invert/pallas_call | solution.py:570
  129.9 2.7 %copy.7 = f32[1536,256]{1,0:T(8,128)} copy(f32[1536,256]{1,0:T(8,128)} %invert.1) | data formatting | bytes 3145728

commit v4 on v3

--- a/solution.py
+++ b/solution.py
@@ -12,8 +12,8 @@
 LOAD = 256
 TURN_LAG = 0
 GROUPS = 4
-CELL_AT = (0, 3, 6, 9, 12, 15)
-BACK_LAG = 1
+CELL_AT = (0, 4, 7, 10, 13, 16)
+BACK_LAG = 0
 DP_AT = (0, 2, 5, 7)
 PIECES = 4
 HALO_LAG = 0

time: 133 us -> 131 us (0.985)
  Pallas kernels: 129 us -> 127 us
    pallas_call x1, Pallas kernels: 129 us -> 127 us  [invert(): pl.pallas_call(functools.partial(body, (n_dp, n_cells), plane), out_shape...]
where the time goes in v4:
time: 131 us
  Pallas kernels  127 us (97%)
  local copies, waits for them, and re-layouts  3.95 us (3%)
    pallas_call x1, Pallas kernels, invert(): pl.pallas_call(functools.partial(body, (n_dp, n_cells), plane), out_shape...  127 us
    unnamed x1, local copies, waits for them, and re-layouts  2.65 us

profile of v4, /device:TPU:0, one launch (start us, length us, event | category | flops | bytes accessed | tf_op | source)
XLA Modules:
  0.0 131.0 jit_solution(1752028217684373937)
XLA Ops:
  0.0 1.3 broadcast_in_dim.3.mask_ref
  1.3 127.0 %invert.1 = f32[1536,256]{1,0:T(8,128)} custom-call(f32[2048,1536]{1,0:T(8,128)} %sens_hbm.1, f32[2048,256]{1,0:T(8,128)} %obs_hbm.1, f32[1536,256]{1,0:T(8,128)} %models_hbm.1, s32[4,768]{1,0:T(4,128)} %near_ref.1, s32[1,1536]{1,0:T(1,128)} %broadcast_in_dim.3.mask_ref), custom_call_target="tpu_custom_call" | custom-call | tf_op jit(solution)/shard_map/invert/pallas_call | solution.py:570
  128.3 2.7 %copy.7 = f32[1536,256]{1,0:T(8,128)} copy(f32[1536,256]{1,0:T(8,128)} %invert.1) | data formatting | bytes 3145728

commit v5 on v4

--- a/solution.py
+++ b/solution.py
@@ -432,9 +432,9 @@
             t_low[:, at] = s_low[at, :].T
 
     def sight(step, g, c):
-        @pl.when((step == 0) & (lax.rem(g, per) == 0))
-        def _():
-            p = lax.div(g, per)
+        @pl.when((step == 0) & (g < pairs))
+        def _():
+            p = g
 
             @pl.when(c == 0)
             def _():
@@ -443,7 +443,7 @@
             at = lanes(c * rows, rows)
             turned = obs_raw[at, lanes(p * LANES, LANES)].T
             for i in range(per):
-                obs[g + i, :, at] = turned[i * width:(i + 1) * width]
+                obs[p * per + i, :, at] = turned[i * width:(i + 1) * width]
 
     def back(step, g, c):
         @pl.when(c == 0)

time: 131 us -> 131 us (level)
  no operation moved by 1% of the time
where the time goes in v5:
time: 131 us
  Pallas kernels  127 us (97%)
  local copies, waits for them, and re-layouts  3.95 us (3%)
    pallas_call x1, Pallas kernels, invert(): pl.pallas_call(functools.partial(body, (n_dp, n_cells), plane), out_shape...  127 us
    unnamed x1, local copies, waits for them, and re-layouts  2.65 us

profile of v5, /device:TPU:0, one launch (start us, length us, event | category | flops | bytes accessed | tf_op | source)
XLA Modules:
  0.0 131.1 jit_solution(16527391235122850217)
XLA Ops:
  0.0 1.3 broadcast_in_dim.3.mask_ref
  1.3 127.2 %invert.1 = f32[1536,256]{1,0:T(8,128)} custom-call(f32[2048,1536]{1,0:T(8,128)} %sens_hbm.1, f32[2048,256]{1,0:T(8,128)} %obs_hbm.1, f32[1536,256]{1,0:T(8,128)} %models_hbm.1, s32[4,768]{1,0:T(4,128)} %near_ref.1, s32[1,1536]{1,0:T(1,128)} %broadcast_in_dim.3.mask_ref), custom_call_target="tpu_custom_call" | custom-call | tf_op jit(solution)/shard_map/invert/pallas_call | solution.py:570
  128.5 2.7 %copy.7 = f32[1536,256]{1,0:T(8,128)} copy(f32[1536,256]{1,0:T(8,128)} %invert.1) | data formatting | bytes 3145728
